TPU v7x, 128 devices: a whole 4x4x4 slice. The times are simulated.
128 devices in a mesh: row: 16 (over z_hi, y, core), col: 8 (over z_lo, x).
Axes of the slice: x: 4, y: 4, z: 4 (z_hi: 2, z_lo: 2; z = z_hi * 2 + z_lo), core: 2. Of those that a mesh axis runs over, the one named last changes fastest.
Arguments:
- multispectral: bfloat16 [2, 32768, 4096], P(None, 'row', 'col'), may hold values from -6 to 6
- hyperspectral: bfloat16 [96, 8192, 1024], P(None, 'row', 'col'), may hold values from -6 to 6
- row_start: float32 [32768, 128], P(('row', 'col')), may hold values from -6 to 6
- col_factor: bfloat16 [4096, 128], P('col', 'row'), may hold values from -0.09375 to 0.09375
- band_factor: float32 [96, 128], replicated, may hold values from -2 to 2
- response: float32 [2, 96], replicated, may hold values from 0.2 to 1
- blur_taps: float32 [9], replicated, may hold values from 0.2 to 1
- offsets: int32 [9], replicated, may hold values from -8 to 8, as said below
Outputs:
- row_factor: float32 [32768, 128], P(('row', 'col'))
- residual: float32 [32768, 128], P(('row', 'col'))
Inputs may be any that keep to these rules, and one draw needn't show every extreme that they name: 9 distinct offsets; -8 and 8 are always among them.
All inputs are finite; a program needn't handle non-finite values.
Results may differ from a plain program's by a relative error of at most 0.0023.
Values may be sent and summed in bfloat16 or wider, within the bound.
A program may use at most 128 MiB of HBM per device.

v0:
```python
import jax
import jax.numpy as jnp
from jax import lax
from jax.sharding import PartitionSpec as P

DEC = 4
W = 8
ITERS = 4
RIDGE_TERM = 0.1
FULL_PRECISION = lax.Precision.HIGHEST


def extended(cells, sides, width):
    for axis, dim in sides:
        count = lax.axis_size(axis)
        head = lax.slice_in_dim(cells, 0, width, axis=dim)
        tail = lax.slice_in_dim(cells, cells.shape[dim] - width, cells.shape[dim], axis=dim)
        cells = jnp.concatenate(
            [
                lax.ppermute(tail, axis, [(i, (i + 1) % count) for i in range(count)]),
                cells,
                lax.ppermute(head, axis, [((i + 1) % count, i) for i in range(count)]),
            ],
            axis=dim,
        )
    return cells


def tap_places(offsets):
    reach = offsets + W
    return (reach // DEC, reach % DEC)


def blur_down(wide, weights, offsets, rows_out):
    shifts, phases = tap_places(offsets)
    quads = wide.reshape(wide.shape[0] // DEC, DEC, wide.shape[1])
    total = jnp.zeros((rows_out, wide.shape[1]), jnp.float32)
    for number in range(weights.shape[0]):
        piece = lax.dynamic_slice(
            quads, (shifts[number], phases[number], 0), (rows_out, 1, wide.shape[1])
        )[:, 0, :]
        total = total + weights[number] * piece.astype(jnp.float32)
    return total


def blur_up(coarse_wide, weights, offsets, margin):
    shifts, phases = tap_places(offsets)
    rows = coarse_wide.shape[0] - 2 * margin
    columns = coarse_wide.shape[1]
    parts = [jnp.zeros((rows, columns), jnp.float32) for _ in range(DEC)]
    for number in range(weights.shape[0]):
        piece = lax.dynamic_slice_in_dim(coarse_wide, margin + 2 - shifts[number], rows, 0)
        for phase in range(DEC):
            scale = jnp.where(phases[number] == phase, weights[number], jnp.float32(0.0))
            parts[phase] = parts[phase] + scale * piece
    return jnp.stack(parts, axis=1).reshape(rows * DEC, columns)


def body(
    multispectral, hyperspectral, row_start, col_factor, band_factor, response, blur_taps, offsets
):
    low_reach = (W + DEC - 1) // DEC
    columns = lax.all_gather(col_factor, "row", axis=1, tiled=True)
    column_wide = extended(columns, (("col", 0),), W)
    coarse_columns = blur_down(column_wide, blur_taps, offsets, columns.shape[0] // DEC)
    merged = jnp.dot(response, band_factor, precision=FULL_PRECISION)
    multi_pairs = (merged[:, None, :] * columns.astype(jnp.float32)[None, :, :]).astype(
        jnp.bfloat16
    )
    hyper_pairs = (band_factor[:, None, :] * coarse_columns[None, :, :]).astype(jnp.bfloat16)
    multi_part = jnp.einsum(
        "kij,kjr->ir", multispectral, multi_pairs, preferred_element_type=jnp.float32
    )
    hyper_part = jnp.einsum(
        "kij,kjr->ir", hyperspectral, hyper_pairs, preferred_element_type=jnp.float32
    )
    column_part = jnp.einsum("jr,js->rs", columns, columns, preferred_element_type=jnp.float32)
    coarse_part = jnp.einsum("jr,js->rs", coarse_columns, coarse_columns, precision=FULL_PRECISION)
    column_gram, coarse_gram = lax.psum((column_part, coarse_part), "col")
    band_gram = jnp.dot(band_factor.T, band_factor, precision=FULL_PRECISION)
    merged_gram = jnp.dot(merged.T, merged, precision=FULL_PRECISION)
    hyper_gram = coarse_gram * band_gram
    multi_gram = column_gram * merged_gram
    multi_sums, hyper_sums = lax.psum((multi_part, hyper_part), "col")
    start_rows = lax.all_gather(row_start, "col", axis=0, tiled=True)

    def inner_sum(first_field, second_field):
        return lax.psum(jnp.sum(first_field * second_field), "row")

    fine_rows = start_rows.shape[0]
    coarse_rows = fine_rows // DEC
    fine_reach = W + DEC * low_reach

    def operate(values):
        fine_wide = extended(values, (("row", 0),), fine_reach)
        coarse_wide = blur_down(fine_wide, blur_taps, offsets, coarse_rows + 2 * low_reach)
        restored = blur_up(coarse_wide, blur_taps, offsets, low_reach)
        return (
            jnp.dot(restored, hyper_gram, precision=FULL_PRECISION)
            + jnp.dot(values, multi_gram, precision=FULL_PRECISION)
            + RIDGE_TERM * values
        )

    hyper_wide = extended(hyper_sums, (("row", 0),), low_reach)
    right_side = blur_up(hyper_wide, blur_taps, offsets, low_reach) + multi_sums
    solution = start_rows
    residual = right_side - operate(solution)
    direction = residual
    norm_now = inner_sum(residual, residual)
    for iteration in range(ITERS):
        mapped = operate(direction)
        step_size = norm_now / inner_sum(direction, mapped)
        solution = solution + step_size * direction
        residual = residual - step_size * mapped
        norm_next = inner_sum(residual, residual)
        direction = residual + norm_next / norm_now * direction
        norm_now = norm_next
    portion = solution.shape[0] // lax.axis_size("col")
    corner = lax.axis_index("col") * portion
    solution = lax.dynamic_slice_in_dim(solution, corner, portion, 0)
    residual = lax.dynamic_slice_in_dim(residual, corner, portion, 0)
    return (solution, residual)


def solution(mesh):
    in_specs = (
        P(None, "row", "col"),
        P(None, "row", "col"),
        P(("row", "col"), None),
        P("col", "row"),
        P(),
        P(),
        P(),
        P(),
    )
    out_specs = (P(("row", "col"), None), P(("row", "col"), None))
    return jax.shard_map(body, mesh=mesh, in_specs=in_specs, out_specs=out_specs, check_vma=False)
```

profile of v0, /device:TPU:0, one launch (start us, length us, event | category | flops | bytes accessed | tf_op | source)
XLA Modules:
  0.0 637.7 jit_solution(14981827791086670884)
XLA Ops:
  7.2 25.9 %all_gather.7 = bf16[512,128]{0,1:T(8,128)(2,1)S(1)} all-gather(bf16[512,8]{0,1:T(8,128)(2,1)} %param.11), channel_id=1, replica_groups=mesh['row'=16,'col'=8] {'row'}, dimensions={1}, use_global_device_ids=true | all-gather | bytes 139264 | tf_op jit(solution)/shard_map/all_gather | solution.py:63
  33.3 1.6 collective-permute-start
  34.9 2.6 collective-permute-start.1
  56.8 4.7 convolution_bitcast_fusion.1
  80.9 5.6 add_bitcast_fusion.4
  87.5 8.2 %fusion.10 = f32[512,128]{0,1:T(8,128)} fusion(bf16[96,512,128]{2,1,0:T(8,128)(2,1)} %param.9, f32[128,128]{0,1:T(8,128)S(1)} %copy.270, f32[96,128]{1,0:T(8,128)S(1)} %copy-done.7), kind=kOutput, calls=%fused_computation.17 | convolution fusion | flops 1613758464 | bytes 12959744 | tf_op jit(solution)/shard_map/kij,kjr->ir/dot_general | solution.py:74
  164.5 5.0 all-reduce.4.cloned.1.call-done
  170.5 5.3 collective-permute-start.3
  182.1 28.2 %all-gather.2.cloned.1.call-done = f32[2048,128]{0,1:T(8,128)} async-done(((f32[256,128]{0,1:T(8,128)}), f32[2048,128]{0,1:T(8,128)}) %all-gather.2.cloned.1.call-update) | async-done | bytes 1048592 | tf_op jit(solution)/shard_map/all_gather | solution.py:85
  210.3 1.6 fusion.80
  211.9 5.5 collective-permute-start.5
  220.5 2.3 constant_dynamic-slice_fusion.43
  222.9 5.8 fusion.43
  233.7 5.6 collective-permute-start.7
  239.3 1.7 collective-permute-done.6
  242.3 2.3 constant_dynamic-slice_fusion.29
  244.6 5.8 fusion.35
  253.6 2.0 multiply_reduce_fusion.6
  255.5 39.2 %all-reduce = (f32[]{:T(128)}, f32[]{:T(128)}) all-reduce(f32[]{:T(128)} %get-tuple-element.11, f32[]{:T(128)} %get-tuple-element.10), channel_id=1, replica_groups=mesh['row'=16,'col'=8] {'row'}, use_global_device_ids=true, to_apply=%region_5.6 | all-reduce | flops 2 | bytes 16 | tf_op jit(solution)/shard_map/psum | solution.py:88
  296.9 33.8 %psum.90 = f32[]{:T(128)} all-reduce(f32[]{:T(128)} %multiply_reduce_fusion.5), channel_id=1, replica_groups=mesh['row'=16,'col'=8] {'row'}, use_global_device_ids=true, to_apply=%region_9.10 | all-reduce | flops 1 | bytes 8 | tf_op jit(solution)/shard_map/psum | solution.py:88
  332.3 5.6 collective-permute-start.9
  337.9 1.7 collective-permute-done.8
  341.2 2.6 copy.298
  343.8 7.2 %constant_dynamic-slice_fusion.17 = (f32[516,1,128]{2,1,0:T(1,128)S(1)}, f32[516,1,128]{2,1,0:T(1,128)S(1)}, f32[516,1,128]{2,1,0:T(1,128)S(1)}, f32[516,1,128]{...) fusion(f32[520,4,128]{2,1,0:T(4,128)} %bitcast.340, ...), kind=kLoop, calls=%fused_computation.222 | loop fusion | bytes 4755528 | tf_op jit(solution)/shard_map/dynamic_slice | solution.py:39
  351.0 5.8 fusion.27
  360.0 2.9 multiply_reduce_fusion.4
  362.8 39.2 %psum.91 = f32[]{:T(128)} all-reduce(f32[]{:T(128)} %get-tuple-element.120), channel_id=1, replica_groups=mesh['row'=16,'col'=8] {'row'}, use_global_device_ids=true, to_apply=%region_11.12 | all-reduce | flops 1 | bytes 8 | tf_op jit(solution)/shard_map/psum | solution.py:88
  403.3 3.0 multiply_reduce_fusion.3
  406.3 33.8 %psum.92 = f32[]{:T(128)} all-reduce(f32[]{:T(128)} %get-tuple-element.20), channel_id=1, replica_groups=mesh['row'=16,'col'=8] {'row'}, use_global_device_ids=true, to_apply=%region_13.14 | all-reduce | flops 1 | bytes 8 | tf_op jit(solution)/shard_map/psum | solution.py:88
  441.5 1.4 multiply_add_fusion.1
  443.0 5.8 collective-permute-start.11
  448.8 1.5 collective-permute-done.10
  452.0 2.6 copy.311
  454.6 7.2 %constant_dynamic-slice_fusion.8 = (f32[516,1,128]{2,1,0:T(1,128)S(1)}, f32[516,1,128]{2,1,0:T(1,128)S(1)}, f32[516,1,128]{2,1,0:T(1,128)S(1)}, f32[516,1,128]{2...) fusion(f32[520,4,128]{2,1,0:T(4,128)} %bitcast.341, ...), kind=kLoop, calls=%fused_computation.213 | loop fusion | bytes 4755528 | tf_op jit(solution)/shard_map/dynamic_slice | solution.py:39
  461.9 5.8 fusion.19
  470.8 2.8 multiply_reduce_fusion.2
  473.7 39.2 %psum.93 = f32[]{:T(128)} all-reduce(f32[]{:T(128)} %get-tuple-element.122), channel_id=1, replica_groups=mesh['row'=16,'col'=8] {'row'}, use_global_device_ids=true, to_apply=%region_15.16 | all-reduce | flops 1 | bytes 8 | tf_op jit(solution)/shard_map/psum | solution.py:88
  514.2 3.4 multiply_reduce_fusion.1
  517.6 33.8 %psum.94 = f32[]{:T(128)} all-reduce(f32[]{:T(128)} %get-tuple-element.18), channel_id=1, replica_groups=mesh['row'=16,'col'=8] {'row'}, use_global_device_ids=true, to_apply=%region_17.18 | all-reduce | flops 1 | bytes 8 | tf_op jit(solution)/shard_map/psum | solution.py:88
  552.8 1.4 multiply_add_fusion
  555.9 5.5 collective-permute-start.13
  561.4 2.0 collective-permute-done.12
  563.4 2.3 concatenate.27
  565.7 2.6 copy.324
  568.3 7.2 %constant_dynamic-slice_fusion.44 = (f32[516,1,128]{2,1,0:T(1,128)S(1)}, f32[516,1,128]{2,1,0:T(1,128)S(1)}, f32[516,1,128]{2,1,0:T(1,128)S(1)}, f32[516,1,128]{...) fusion(f32[520,4,128]{2,1,0:T(4,128)} %bitcast.337, ...), kind=kLoop, calls=%fused_computation.249 | loop fusion | bytes 4755528 | tf_op jit(solution)/shard_map/dynamic_slice | solution.py:39
  575.6 5.8 fusion.11
  584.7 2.8 multiply_reduce_fusion
  587.5 39.1 %psum.95 = f32[]{:T(128)} all-reduce(f32[]{:T(128)} %get-tuple-element.124), channel_id=1, replica_groups=mesh['row'=16,'col'=8] {'row'}, use_global_device_ids=true, to_apply=%region_19.20 | all-reduce | flops 1 | bytes 8 | tf_op jit(solution)/shard_map/psum | solution.py:88
  (117 shorter events, 46.0 us)
Async XLA Ops:
  7.2 49.5 %copy-start = (f32[2,96]{1,0:T(2,128)S(1)}, f32[2,96]{1,0:T(2,128)}, u32[]{:S(2)}) copy-start(f32[2,96]{1,0:T(2,128)} %param.13) | copy-start | bytes 2308
  7.2 48.8 %copy-start.9 = (f32[9]{0:T(128)S(1)}, f32[9]{0:T(128)}, u32[]{:S(2)}) copy-start(f32[9]{0:T(128)} %param.14) | copy-start | bytes 112
  7.2 49.5 %copy-start.7 = (f32[96,128]{1,0:T(8,128)S(1)}, f32[96,128]{1,0:T(8,128)}, u32[]{:S(2)}) copy-start(f32[96,128]{1,0:T(8,128)} %param.12) | copy-start | bytes 147460
  7.2 162.3 %all-reduce.4.cloned.1.call-start = ((), (), s32[]{:S(2)}) async-start(), calls=%async_computation.1 | async-start | bytes 2883584 | tf_op jit(solution)/shard_map/psum | solution.py:79
  33.3 46.9 %collective-permute-start = (bf16[8,128]{1,0:T(8,128)(2,1)S(1)}, bf16[8,128]{1,0:T(8,128)(2,1)S(1)}, u32[]{:S(2)}, u32[]{:S(2)}) collective-permute-start(bf16[8,128]{1,0:T(8,128)(2,1)S(1)} %get-tuple-element.90), channel_id=1, source_target_pairs={{0,1},{1,2},{2,3},{3,4},{4,5},{5,6},{6,7},{7,0},{8,9},{9,10},{10,1... | collective-permute-start | bytes 6152 | tf_op jit(solution)/shard_map/ppermute | solution.py:20
  34.9 45.3 %collective-permute-start.1 = (bf16[8,128]{1,0:T(8,128)(2,1)S(1)}, bf16[8,128]{1,0:T(8,128)(2,1)S(1)}, u32[]{:S(2)}, u32[]{:S(2)}) collective-permute-start(bf16[8,128]{1,0:T(8,128)(2,1)S(1)} %get-tuple-element.91), channel_id=1, source_target_pairs={{1,0},{2,1},{3,2},{4,3},{5,4},{6,5},{7,6},{0,7},{9,8},{10,9},{11,1... | collective-permute-start | bytes 6152 | tf_op jit(solution)/shard_map/ppermute | solution.py:22
  95.7 0.9 copy-start.8
  95.7 114.6 %all-gather.2.cloned.1.call-start = ((), (), s32[]{:S(2)}) async-start(), calls=%async_computation | async-start | bytes 1179648 | tf_op jit(solution)/shard_map/all_gather | solution.py:85
  170.5 7.7 %collective-permute-start.2 = (f32[2,128]{0,1:T(8,128)S(1)}, f32[2,128]{0,1:T(8,128)S(1)}, u32[]{:S(2)}, u32[]{:S(2)}) collective-permute-start(f32[2,128]{0,1:T(8,128)S(1)} %get-tuple-element.79), channel_id=1, source_target_pairs={{0,8},{8,16},{16,24},{24,32},{32,40},{40,48},{48,56},{56,64},{64,7... | collective-permute-start | bytes 3080 | tf_op jit(solution)/shard_map/ppermute | solution.py:20
  170.5 7.6 %collective-permute-start.3 = (f32[2,128]{0,1:T(8,128)S(1)}, f32[2,128]{0,1:T(8,128)S(1)}, u32[]{:S(2)}, u32[]{:S(2)}) collective-permute-start(f32[2,128]{0,1:T(8,128)S(1)} %get-tuple-element.80), channel_id=1, source_target_pairs={{8,0},{16,8},{24,16},{32,24},{40,32},{48,40},{56,48},{64,56},{72,6... | collective-permute-start | bytes 3080 | tf_op jit(solution)/shard_map/ppermute | solution.py:22
  211.9 7.5 %collective-permute-start.4 = (f32[16,128]{0,1:T(8,128)}, f32[16,128]{0,1:T(8,128)S(1)}, u32[]{:S(2)}, u32[]{:S(2)}) collective-permute-start(f32[16,128]{0,1:T(8,128)} %get-tuple-element.78), channel_id=1, source_target_pairs={{0,8},{8,16},{16,24},{24,32},{32,40},{40,48},{48,56},{56,64},{64,7... | collective-permute-start | bytes 24584 | tf_op jit(solution)/shard_map/ppermute | solution.py:20
  211.9 7.5 %collective-permute-start.5 = (f32[16,128]{0,1:T(8,128)S(1)}, f32[16,128]{0,1:T(8,128)S(1)}, u32[]{:S(2)}, u32[]{:S(2)}) collective-permute-start(f32[16,128]{0,1:T(8,128)S(1)} %get-tuple-element.77), channel_id=1, source_target_pairs={{8,0},{16,8},{24,16},{32,24},{40,32},{48,40},{56,48},{64,56},{72,6... | collective-permute-start | bytes 24584 | tf_op jit(solution)/shard_map/ppermute | solution.py:22
  217.9 1.6 copy-start.4
  230.7 1.2 copy-start.5
  230.7 1.5 copy-start.6
  233.6 7.3 %collective-permute-start.6 = (f32[16,128]{0,1:T(8,128)S(1)}, f32[16,128]{0,1:T(8,128)S(1)}, u32[]{:S(2)}, u32[]{:S(2)}) collective-permute-start(f32[16,128]{0,1:T(8,128)S(1)} %get-tuple-element.76), channel_id=1, source_target_pairs={{0,8},{8,16},{16,24},{24,32},{32,40},{40,48},{48,56},{56,64},{64,7... | collective-permute-start | bytes 24584 | tf_op jit(solution)/shard_map/ppermute | solution.py:20
  233.7 7.5 %collective-permute-start.7 = (f32[16,128]{0,1:T(8,128)S(1)}, f32[16,128]{0,1:T(8,128)S(1)}, u32[]{:S(2)}, u32[]{:S(2)}) collective-permute-start(f32[16,128]{0,1:T(8,128)S(1)} %get-tuple-element.75), channel_id=1, source_target_pairs={{8,0},{16,8},{24,16},{32,24},{40,32},{48,40},{56,48},{64,56},{72,6... | collective-permute-start | bytes 24584 | tf_op jit(solution)/shard_map/ppermute | solution.py:22
  332.3 7.3 %collective-permute-start.8 = (f32[16,128]{0,1:T(8,128)S(1)}, f32[16,128]{0,1:T(8,128)S(1)}, u32[]{:S(2)}, u32[]{:S(2)}) collective-permute-start(f32[16,128]{0,1:T(8,128)S(1)} %get-tuple-element.74), channel_id=1, source_target_pairs={{0,8},{8,16},{16,24},{24,32},{32,40},{40,48},{48,56},{56,64},{64,7... | collective-permute-start | bytes 24584 | tf_op jit(solution)/shard_map/ppermute | solution.py:20
  332.3 7.5 %collective-permute-start.9 = (f32[16,128]{0,1:T(8,128)S(1)}, f32[16,128]{0,1:T(8,128)S(1)}, u32[]{:S(2)}, u32[]{:S(2)}) collective-permute-start(f32[16,128]{0,1:T(8,128)S(1)} %get-tuple-element.73), channel_id=1, source_target_pairs={{8,0},{16,8},{24,16},{32,24},{40,32},{48,40},{56,48},{64,56},{72,6... | collective-permute-start | bytes 24584 | tf_op jit(solution)/shard_map/ppermute | solution.py:22
  443.0 7.3 %collective-permute-start.10 = (f32[16,128]{0,1:T(8,128)S(1)}, f32[16,128]{0,1:T(8,128)S(1)}, u32[]{:S(2)}, u32[]{:S(2)}) collective-permute-start(f32[16,128]{0,1:T(8,128)S(1)} %get-tuple-element.72), channel_id=1, source_target_pairs={{0,8},{8,16},{16,24},{24,32},{32,40},{40,48},{48,56},{56,64},{64,7... | collective-permute-start | bytes 24584 | tf_op jit(solution)/shard_map/ppermute | solution.py:20
  443.0 7.7 %collective-permute-start.11 = (f32[16,128]{0,1:T(8,128)S(1)}, f32[16,128]{0,1:T(8,128)S(1)}, u32[]{:S(2)}, u32[]{:S(2)}) collective-permute-start(f32[16,128]{0,1:T(8,128)S(1)} %get-tuple-element.71), channel_id=1, source_target_pairs={{8,0},{16,8},{24,16},{32,24},{40,32},{48,40},{56,48},{64,56},{72,6... | collective-permute-start | bytes 24584 | tf_op jit(solution)/shard_map/ppermute | solution.py:22
  554.2 1.0 copy-start.2
  555.9 7.5 %collective-permute-start.12 = (f32[16,128]{0,1:T(8,128)}, f32[16,128]{0,1:T(8,128)S(1)}, u32[]{:S(2)}, u32[]{:S(2)}) collective-permute-start(f32[16,128]{0,1:T(8,128)} %get-tuple-element.70), channel_id=1, source_target_pairs={{0,8},{8,16},{16,24},{24,32},{32,40},{40,48},{48,56},{56,64},{64,7... | collective-permute-start | bytes 24584 | tf_op jit(solution)/shard_map/ppermute | solution.py:20
  555.9 7.5 %collective-permute-start.13 = (f32[16,128]{0,1:T(8,128)S(1)}, f32[16,128]{0,1:T(8,128)S(1)}, u32[]{:S(2)}, u32[]{:S(2)}) collective-permute-start(f32[16,128]{0,1:T(8,128)S(1)} %get-tuple-element.69), channel_id=1, source_target_pairs={{8,0},{16,8},{24,16},{32,24},{40,32},{48,40},{56,48},{64,56},{72,6... | collective-permute-start | bytes 24584 | tf_op jit(solution)/shard_map/ppermute | solution.py:22
  583.4 1.2 copy-start.3
  584.7 46.0 %copy-start.1 = (f32[2,96]{1,0:T(2,128)S(1)}, f32[2,96]{1,0:T(2,128)}, u32[]{:S(2)}) copy-start(f32[2,96]{1,0:T(2,128)} %param.13) | copy-start | bytes 2308
Sparse Core Ops, SparseCore 0:
  95.8 73.6 all-reduce.3
  171.7 38.5 all-gather.1
where the time goes:
time: 648 us; the launch traced here: 638 us
  blocking collectives  284 us (44%)
  between operations  125 us (19%)
  other arithmetic  58.2 us (9%)
  local copies, waits for them, and re-layouts  57.5 us (9%)
  waiting for transfers between devices  41.1 us (6%)
  starting transfers between devices  37.8 us (6%)
  matrix products  34.2 us (5%)
    psum x7, blocking collectives, inner_sum(): return lax.psum(jnp.sum(first_field * second_field), 'row')  258 us
    ppermute x7, starting transfers between devices, extended(): lax.ppermute(head, axis, [((i + 1) % count, i) for i in range(count)])  36 us
    add x6, other arithmetic, blur_down(): total = total + weights[number] * piece.astype(jnp.float32)  34.5 us
    all_gather x1, waiting for transfers between devices, body(): start_rows = lax.all_gather(row_start, 'col', axis=0, tiled=True)  28.2 us
    dynamic_slice x6, local copies, waits for them, and re-layouts, blur_down(): lax.dynamic_slice(quads, (shifts[number], phases[number], 0), (rows_out,...  27 us
    all_gather x1, blocking collectives, body(): columns = lax.all_gather(col_factor, 'row', axis=1, tiled=True)  25.9 us
    concatenate x10, local copies, waits for them, and re-layouts, extended(): jnp.concatenate([lax.ppermute(tail, axis, [(i, (i + 1) % count) for i in...  14.9 us
  transfers between devices with their start and end apart: 16, of which 10 were waited for; matrix products, arithmetic and copies ran while one was open for 3% of the time, Pallas kernels for 0%

commit v1 on v0

--- a/solution.py
+++ b/solution.py
@@ -82,7 +82,9 @@
     hyper_gram = coarse_gram * band_gram
     multi_gram = column_gram * merged_gram
     multi_sums, hyper_sums = lax.psum((multi_part, hyper_part), "col")
-    start_rows = lax.all_gather(row_start, "col", axis=0, tiled=True)
+    start_rows = jnp.concatenate(
+        lax.all_to_all(jnp.stack([row_start] * lax.axis_size("col")), "col", 0, 0), axis=0
+    )
 
     def inner_sum(first_field, second_field):
         return lax.psum(jnp.sum(first_field * second_field), "row")

time: 648 us -> 618 us (0.954)
  waiting for transfers between devices: 41.1 us -> 7.7 us
    all_gather x1 -> x0, waiting for transfers between devices: 28.2 us -> none  [body(): start_rows = lax.all_gather(row_start, 'col', axis=0, tiled=True)]
  transfers between devices with their start and end apart: 16 -> 16, of which waited for: 10 -> 7; matrix products, arithmetic and copies ran while one was open for 3% -> 7% of each run, Pallas kernels for 0% -> 0%
where the time goes in v1:
time: 618 us; the launch traced here: 607 us
  blocking collectives  284 us (46%)
  between operations  125 us (20%)
  local copies, waits for them, and re-layouts  56.1 us (9%)
  other arithmetic  56.1 us (9%)
  starting transfers between devices  41.4 us (7%)
  matrix products  36.2 us (6%)
  waiting for transfers between devices  7.7 us (1%)
    psum x7, blocking collectives, inner_sum(): return lax.psum(jnp.sum(first_field * second_field), 'row')  258 us
    ppermute x7, starting transfers between devices, extended(): lax.ppermute(head, axis, [((i + 1) % count, i) for i in range(count)])  35.9 us
    add x6, other arithmetic, blur_down(): total = total + weights[number] * piece.astype(jnp.float32)  34.6 us
    dynamic_slice x6, local copies, waits for them, and re-layouts, blur_down(): lax.dynamic_slice(quads, (shifts[number], phases[number], 0), (rows_out,...  27 us
    all_gather x1, blocking collectives, body(): columns = lax.all_gather(col_factor, 'row', axis=1, tiled=True)  25.9 us
    concatenate x10, local copies, waits for them, and re-layouts, extended(): jnp.concatenate([lax.ppermute(tail, axis, [(i, (i + 1) % count) for i in...  15 us
    dot_general x5, matrix products, operate(): jnp.dot(values, multi_gram, precision=FULL_PRECISION)  13.7 us
  transfers between devices with their start and end apart: 16, of which 7 were waited for; matrix products, arithmetic and copies ran while one was open for 7% of the time, Pallas kernels for 0%

profile of v1, /device:TPU:0, one launch (start us, length us, event | category | flops | bytes accessed | tf_op | source)
XLA Modules:
  0.0 606.7 jit_solution(4827874159508360752)
XLA Ops:
  7.2 25.9 %all_gather.3 = bf16[512,128]{0,1:T(8,128)(2,1)S(1)} all-gather(bf16[512,8]{0,1:T(8,128)(2,1)} %param.11), channel_id=1, replica_groups=mesh['row'=16,'col'=8] {'row'}, dimensions={1}, use_global_device_ids=true | all-gather | bytes 139264 | tf_op jit(solution)/shard_map/all_gather | solution.py:63
  33.2 1.6 collective-permute-start
  34.8 2.6 collective-permute-start.1
  39.5 3.7 all-to-all-start
  61.5 4.7 convolution_bitcast_fusion.1
  85.4 5.7 add_bitcast_fusion.4
  92.1 8.2 %fusion.10 = f32[512,128]{0,1:T(8,128)} fusion(bf16[96,512,128]{2,1,0:T(8,128)(2,1)} %param.9, f32[128,128]{0,1:T(8,128)S(1)} %copy.272, f32[96,128]{1,0:T(8,128)S(1)} %copy-done.6), kind=kOutput, calls=%fused_computation.17 | convolution fusion | flops 1613758464 | bytes 12959744 | tf_op jit(solution)/shard_map/kij,kjr->ir/dot_general | solution.py:74
  100.6 5.3 collective-permute-start.5
  174.3 2.3 constant_dynamic-slice_fusion.43
  176.7 5.8 fusion.43
  185.6 5.5 collective-permute-start.3
  192.3 2.1 fusion.88
  199.5 3.1 fusion.5
  202.8 5.7 collective-permute-start.7
  208.5 1.6 collective-permute-done.6
  211.5 2.3 constant_dynamic-slice_fusion.29
  213.9 5.8 fusion.35
  222.8 2.0 multiply_reduce_fusion.6
  224.8 39.2 %all-reduce = (f32[]{:T(128)}, f32[]{:T(128)}) all-reduce(f32[]{:T(128)} %get-tuple-element.11, f32[]{:T(128)} %get-tuple-element.10), channel_id=1, replica_groups=mesh['row'=16,'col'=8] {'row'}, use_global_device_ids=true, to_apply=%region_5.6 | all-reduce | flops 2 | bytes 16 | tf_op jit(solution)/shard_map/psum | solution.py:90
  266.2 33.8 %psum.90 = f32[]{:T(128)} all-reduce(f32[]{:T(128)} %multiply_reduce_fusion.5), channel_id=1, replica_groups=mesh['row'=16,'col'=8] {'row'}, use_global_device_ids=true, to_apply=%region_9.10 | all-reduce | flops 1 | bytes 8 | tf_op jit(solution)/shard_map/psum | solution.py:90
  301.6 5.5 collective-permute-start.9
  307.1 1.8 collective-permute-done.8
  310.4 2.6 copy.300
  313.0 7.2 %constant_dynamic-slice_fusion.17 = (f32[516,1,128]{2,1,0:T(1,128)S(1)}, f32[516,1,128]{2,1,0:T(1,128)S(1)}, f32[516,1,128]{2,1,0:T(1,128)S(1)}, f32[516,1,128]{...) fusion(f32[520,4,128]{2,1,0:T(4,128)} %bitcast.342, ...), kind=kLoop, calls=%fused_computation.222 | loop fusion | bytes 4755528 | tf_op jit(solution)/shard_map/dynamic_slice | solution.py:39
  320.2 5.8 fusion.27
  329.1 2.9 multiply_reduce_fusion.4
  332.0 39.2 %psum.91 = f32[]{:T(128)} all-reduce(f32[]{:T(128)} %get-tuple-element.120), channel_id=1, replica_groups=mesh['row'=16,'col'=8] {'row'}, use_global_device_ids=true, to_apply=%region_11.12 | all-reduce | flops 1 | bytes 8 | tf_op jit(solution)/shard_map/psum | solution.py:90
  372.5 3.0 multiply_reduce_fusion.3
  375.5 33.8 %psum.92 = f32[]{:T(128)} all-reduce(f32[]{:T(128)} %get-tuple-element.20), channel_id=1, replica_groups=mesh['row'=16,'col'=8] {'row'}, use_global_device_ids=true, to_apply=%region_13.14 | all-reduce | flops 1 | bytes 8 | tf_op jit(solution)/shard_map/psum | solution.py:90
  410.6 1.4 multiply_add_fusion.1
  412.2 5.5 collective-permute-start.11
  417.7 1.8 collective-permute-done.10
  421.0 2.6 copy.313
  423.6 7.2 %constant_dynamic-slice_fusion.8 = (f32[516,1,128]{2,1,0:T(1,128)S(1)}, f32[516,1,128]{2,1,0:T(1,128)S(1)}, f32[516,1,128]{2,1,0:T(1,128)S(1)}, f32[516,1,128]{2...) fusion(f32[520,4,128]{2,1,0:T(4,128)} %bitcast.343, ...), kind=kLoop, calls=%fused_computation.213 | loop fusion | bytes 4755528 | tf_op jit(solution)/shard_map/dynamic_slice | solution.py:39
  430.8 5.8 fusion.19
  439.7 2.8 multiply_reduce_fusion.2
  442.6 39.2 %psum.93 = f32[]{:T(128)} all-reduce(f32[]{:T(128)} %get-tuple-element.122), channel_id=1, replica_groups=mesh['row'=16,'col'=8] {'row'}, use_global_device_ids=true, to_apply=%region_15.16 | all-reduce | flops 1 | bytes 8 | tf_op jit(solution)/shard_map/psum | solution.py:90
  483.1 3.4 multiply_reduce_fusion.1
  486.5 33.8 %psum.94 = f32[]{:T(128)} all-reduce(f32[]{:T(128)} %get-tuple-element.18), channel_id=1, replica_groups=mesh['row'=16,'col'=8] {'row'}, use_global_device_ids=true, to_apply=%region_17.18 | all-reduce | flops 1 | bytes 8 | tf_op jit(solution)/shard_map/psum | solution.py:90
  521.6 1.4 multiply_add_fusion
  524.7 5.6 collective-permute-start.13
  530.3 1.9 collective-permute-done.12
  532.2 2.3 concatenate.27
  534.5 2.6 copy.326
  537.1 7.2 %constant_dynamic-slice_fusion.44 = (f32[516,1,128]{2,1,0:T(1,128)S(1)}, f32[516,1,128]{2,1,0:T(1,128)S(1)}, f32[516,1,128]{2,1,0:T(1,128)S(1)}, f32[516,1,128]{...) fusion(f32[520,4,128]{2,1,0:T(4,128)} %bitcast.339, ...), kind=kLoop, calls=%fused_computation.249 | loop fusion | bytes 4755528 | tf_op jit(solution)/shard_map/dynamic_slice | solution.py:39
  544.3 5.8 fusion.11
  553.4 2.8 multiply_reduce_fusion
  556.2 39.1 %psum.95 = f32[]{:T(128)} all-reduce(f32[]{:T(128)} %get-tuple-element.124), channel_id=1, replica_groups=mesh['row'=16,'col'=8] {'row'}, use_global_device_ids=true, to_apply=%region_19.20 | all-reduce | flops 1 | bytes 8 | tf_op jit(solution)/shard_map/psum | solution.py:90
  (118 shorter events, 40.5 us)
Async XLA Ops:
  7.2 54.2 %copy-start = (f32[2,96]{1,0:T(2,128)S(1)}, f32[2,96]{1,0:T(2,128)}, u32[]{:S(2)}) copy-start(f32[2,96]{1,0:T(2,128)} %param.13) | copy-start | bytes 2308
  33.2 51.4 %collective-permute-start = (bf16[8,128]{1,0:T(8,128)(2,1)S(1)}, bf16[8,128]{1,0:T(8,128)(2,1)S(1)}, u32[]{:S(2)}, u32[]{:S(2)}) collective-permute-start(bf16[8,128]{1,0:T(8,128)(2,1)S(1)} %get-tuple-element.90), channel_id=1, source_target_pairs={{0,1},{1,2},{2,3},{3,4},{4,5},{5,6},{6,7},{7,0},{8,9},{9,10},{10,1... | collective-permute-start | bytes 6152 | tf_op jit(solution)/shard_map/ppermute | solution.py:20
  34.8 49.9 %collective-permute-start.1 = (bf16[8,128]{1,0:T(8,128)(2,1)S(1)}, bf16[8,128]{1,0:T(8,128)(2,1)S(1)}, u32[]{:S(2)}, u32[]{:S(2)}) collective-permute-start(bf16[8,128]{1,0:T(8,128)(2,1)S(1)} %get-tuple-element.91), channel_id=1, source_target_pairs={{1,0},{2,1},{3,2},{4,3},{5,4},{6,5},{7,6},{0,7},{9,8},{10,9},{11,1... | collective-permute-start | bytes 6152 | tf_op jit(solution)/shard_map/ppermute | solution.py:22
  39.5 3.8 copy-start.9
  39.5 21.2 %copy-start.8 = (f32[9]{0:T(128)S(1)}, f32[9]{0:T(128)}, u32[]{:S(2)}) copy-start(f32[9]{0:T(128)} %param.14) | copy-start | bytes 112
  39.5 21.9 %copy-start.6 = (f32[96,128]{1,0:T(8,128)S(1)}, f32[96,128]{1,0:T(8,128)}, u32[]{:S(2)}) copy-start(f32[96,128]{1,0:T(8,128)} %param.12) | copy-start | bytes 147460
  39.5 60.8 %all-to-all-start = ((f32[8,256,128]{1,2,0:T(8,128)}), f32[8,256,128]{1,2,0:T(8,128)S(1)}, u32[]{:S(2)}, u32[]{:S(2)}) async-start(f32[8,256,128]{1,2,0:T(8,128)} %stack.101), calls=%async_computation | async-start | bytes 2097152 | tf_op jit(solution)/shard_map/all_to_all | solution.py:86
  43.2 141.4 %all-reduce.4.cloned.1.call-start = ((), (), s32[]{:S(2)}) async-start(), calls=%async_computation.1 | async-start | bytes 2883584 | tf_op jit(solution)/shard_map/psum | solution.py:79
  100.4 99.1 %copy-start.4 = (f32[8,16,8,256]{3,2,0,1:T(8,128)}, f32[8,16,8,256]{3,2,0,1:T(8,128)S(1)}, u32[]{:S(2)}) copy-start(f32[8,16,8,256]{3,2,0,1:T(8,128)S(1)} %copy.404) | copy-start | bytes 3145732
  100.5 72.7 %collective-permute-start.4 = (f32[16,128]{0,1:T(8,128)S(1)}, f32[16,128]{0,1:T(8,128)S(1)}, u32[]{:S(2)}, u32[]{:S(2)}) collective-permute-start(f32[16,128]{0,1:T(8,128)S(1)} %get-tuple-element.78), channel_id=1, source_target_pairs={{0,8},{8,16},{16,24},{24,32},{32,40},{40,48},{48,56},{56,64},{64,7... | collective-permute-start | bytes 24584 | tf_op jit(solution)/shard_map/ppermute | solution.py:20
  100.6 72.6 %collective-permute-start.5 = (f32[16,128]{0,1:T(8,128)S(1)}, f32[16,128]{0,1:T(8,128)S(1)}, u32[]{:S(2)}, u32[]{:S(2)}) collective-permute-start(f32[16,128]{0,1:T(8,128)S(1)} %get-tuple-element.77), channel_id=1, source_target_pairs={{8,0},{16,8},{24,16},{32,24},{40,32},{48,40},{56,48},{64,56},{72,6... | collective-permute-start | bytes 24584 | tf_op jit(solution)/shard_map/ppermute | solution.py:22
  185.5 9.1 %collective-permute-start.2 = (f32[2,128]{0,1:T(8,128)S(1)}, f32[2,128]{0,1:T(8,128)S(1)}, u32[]{:S(2)}, u32[]{:S(2)}) collective-permute-start(f32[2,128]{0,1:T(8,128)S(1)} %get-tuple-element.79), channel_id=1, source_target_pairs={{0,8},{8,16},{16,24},{24,32},{32,40},{40,48},{48,56},{56,64},{64,7... | collective-permute-start | bytes 3080 | tf_op jit(solution)/shard_map/ppermute | solution.py:20
  185.6 9.1 %collective-permute-start.3 = (f32[2,128]{0,1:T(8,128)S(1)}, f32[2,128]{0,1:T(8,128)S(1)}, u32[]{:S(2)}, u32[]{:S(2)}) collective-permute-start(f32[2,128]{0,1:T(8,128)S(1)} %get-tuple-element.80), channel_id=1, source_target_pairs={{8,0},{16,8},{24,16},{32,24},{40,32},{48,40},{56,48},{64,56},{72,6... | collective-permute-start | bytes 3080 | tf_op jit(solution)/shard_map/ppermute | solution.py:22
  192.3 2.1 copy-start.7
  192.3 2.4 copy-start.5
  202.7 7.3 %collective-permute-start.6 = (f32[16,128]{0,1:T(8,128)S(1)}, f32[16,128]{0,1:T(8,128)S(1)}, u32[]{:S(2)}, u32[]{:S(2)}) collective-permute-start(f32[16,128]{0,1:T(8,128)S(1)} %get-tuple-element.76), channel_id=1, source_target_pairs={{0,8},{8,16},{16,24},{24,32},{32,40},{40,48},{48,56},{56,64},{64,7... | collective-permute-start | bytes 24584 | tf_op jit(solution)/shard_map/ppermute | solution.py:20
  202.8 7.6 %collective-permute-start.7 = (f32[16,128]{0,1:T(8,128)S(1)}, f32[16,128]{0,1:T(8,128)S(1)}, u32[]{:S(2)}, u32[]{:S(2)}) collective-permute-start(f32[16,128]{0,1:T(8,128)S(1)} %get-tuple-element.75), channel_id=1, source_target_pairs={{8,0},{16,8},{24,16},{32,24},{40,32},{48,40},{56,48},{64,56},{72,6... | collective-permute-start | bytes 24584 | tf_op jit(solution)/shard_map/ppermute | solution.py:22
  301.6 7.3 %collective-permute-start.8 = (f32[16,128]{0,1:T(8,128)S(1)}, f32[16,128]{0,1:T(8,128)S(1)}, u32[]{:S(2)}, u32[]{:S(2)}) collective-permute-start(f32[16,128]{0,1:T(8,128)S(1)} %get-tuple-element.74), channel_id=1, source_target_pairs={{0,8},{8,16},{16,24},{24,32},{32,40},{40,48},{48,56},{56,64},{64,7... | collective-permute-start | bytes 24584 | tf_op jit(solution)/shard_map/ppermute | solution.py:20
  301.6 7.4 %collective-permute-start.9 = (f32[16,128]{0,1:T(8,128)S(1)}, f32[16,128]{0,1:T(8,128)S(1)}, u32[]{:S(2)}, u32[]{:S(2)}) collective-permute-start(f32[16,128]{0,1:T(8,128)S(1)} %get-tuple-element.73), channel_id=1, source_target_pairs={{8,0},{16,8},{24,16},{32,24},{40,32},{48,40},{56,48},{64,56},{72,6... | collective-permute-start | bytes 24584 | tf_op jit(solution)/shard_map/ppermute | solution.py:22
  412.1 7.3 %collective-permute-start.10 = (f32[16,128]{0,1:T(8,128)S(1)}, f32[16,128]{0,1:T(8,128)S(1)}, u32[]{:S(2)}, u32[]{:S(2)}) collective-permute-start(f32[16,128]{0,1:T(8,128)S(1)} %get-tuple-element.72), channel_id=1, source_target_pairs={{0,8},{8,16},{16,24},{24,32},{32,40},{40,48},{48,56},{56,64},{64,7... | collective-permute-start | bytes 24584 | tf_op jit(solution)/shard_map/ppermute | solution.py:20
  412.2 7.4 %collective-permute-start.11 = (f32[16,128]{0,1:T(8,128)S(1)}, f32[16,128]{0,1:T(8,128)S(1)}, u32[]{:S(2)}, u32[]{:S(2)}) collective-permute-start(f32[16,128]{0,1:T(8,128)S(1)} %get-tuple-element.71), channel_id=1, source_target_pairs={{8,0},{16,8},{24,16},{32,24},{40,32},{48,40},{56,48},{64,56},{72,6... | collective-permute-start | bytes 24584 | tf_op jit(solution)/shard_map/ppermute | solution.py:22
  523.0 1.0 copy-start.2
  524.7 7.5 %collective-permute-start.12 = (f32[16,128]{0,1:T(8,128)}, f32[16,128]{0,1:T(8,128)S(1)}, u32[]{:S(2)}, u32[]{:S(2)}) collective-permute-start(f32[16,128]{0,1:T(8,128)} %get-tuple-element.70), channel_id=1, source_target_pairs={{0,8},{8,16},{16,24},{24,32},{32,40},{40,48},{48,56},{56,64},{64,7... | collective-permute-start | bytes 24584 | tf_op jit(solution)/shard_map/ppermute | solution.py:20
  524.7 7.5 %collective-permute-start.13 = (f32[16,128]{0,1:T(8,128)S(1)}, f32[16,128]{0,1:T(8,128)S(1)}, u32[]{:S(2)}, u32[]{:S(2)}) collective-permute-start(f32[16,128]{0,1:T(8,128)S(1)} %get-tuple-element.69), channel_id=1, source_target_pairs={{8,0},{16,8},{24,16},{32,24},{40,32},{48,40},{56,48},{64,56},{72,6... | collective-permute-start | bytes 24584 | tf_op jit(solution)/shard_map/ppermute | solution.py:22
  552.2 1.2 copy-start.3
  553.4 46.0 %copy-start.1 = (f32[2,96]{1,0:T(2,128)S(1)}, f32[2,96]{1,0:T(2,128)}, u32[]{:S(2)}) copy-start(f32[2,96]{1,0:T(2,128)} %param.13) | copy-start | bytes 2308
Sparse Core Ops, SparseCore 0:
  100.4 76.6 all-reduce.3
